TPU v7x, 512 devices: a whole 4x8x8 slice. The times are simulated.
512 devices in a mesh: section: 2 (over core), tm: 32 (over x, z), tile: 8 (over y).
Axes of the slice: x: 4, y: 8, z: 8, core: 2. Of those that a mesh axis runs over, the one named last changes fastest.
Arguments:
- features: bfloat16 [64, 64, 64, 256], P('tm', 'tile', None, 'section'), may hold values from -320 to 320
- norm_gain_in: float32 [256], replicated, may hold values from 0.1 to 1.9
- norm_shift_in: float32 [256], replicated, may hold values from -0.8 to 0.8
- conv_in_weight: bfloat16 [3, 3, 3, 256, 128], replicated, may hold values from -0.078125 to 0.078125
- conv_in_bias: float32 [128], replicated, may hold values from -1 to 1
- norm_gain_mid: float32 [128], replicated, may hold values from 0.1 to 1.9
- norm_shift_mid: float32 [128], replicated, may hold values from -0.8 to 0.8
- conv_mid_weight: bfloat16 [3, 3, 3, 128, 128], replicated, may hold values from -0.109375 to 0.109375
- conv_mid_bias: float32 [128], replicated, may hold values from -0.6 to 0.6
- skip_weight: bfloat16 [256, 128], replicated, may hold values from -0.09375 to 0.09375
- skip_bias: float32 [128], replicated, may hold values from -0.6 to 0.6
Outputs:
- block_out: bfloat16 [64, 64, 64, 128], P('tm', 'tile', 'section')
All inputs are finite; a program needn't handle non-finite values.
Results may differ from a plain program's by a relative error of at most 0.008.
Values may be sent and summed in bfloat16 or wider, within the bound.
A program may use at most 64 MiB of HBM per device.

v0:
```python
import jax
import jax.numpy as jnp
from jax import lax
from jax.sharding import PartitionSpec as P

GROUPS = 32


def passed_along(value, axis, steps):
    count = lax.axis_size(axis)
    leading, last = (max(0, -steps), min(count, count - steps))
    return lax.ppermute(value, axis, [(source, source + steps) for source in range(leading, last)])


def with_halo(cells, sides, width):
    for axis, dim in sides:
        count = lax.axis_size(axis)
        ends = count - 1
        head = lax.slice_in_dim(cells, 0, width, axis=dim)
        tail = lax.slice_in_dim(cells, cells.shape[dim] - width, cells.shape[dim], axis=dim)
        cells = jnp.concatenate(
            [
                lax.ppermute(tail, axis, [(i, (i + 1) % count) for i in range(ends)]),
                cells,
                lax.ppermute(head, axis, [((i + 1) % count, i) for i in range(ends)]),
            ],
            axis=dim,
        )
    return cells


def group_stats(values, total_cells):
    channels = values.shape[-1]
    grouped = values.reshape(-1, GROUPS, channels // GROUPS)
    cell_count = total_cells * (channels // GROUPS)
    group_mean = lax.psum(jnp.sum(grouped, axis=(0, 2)), ("section", "tm", "tile")) / cell_count
    centered = grouped - group_mean[None, :, None]
    spread = (
        lax.psum(jnp.sum(centered * centered, axis=(0, 2)), ("section", "tm", "tile")) / cell_count
    )
    inv_scale = lax.rsqrt(spread + 1e-06)
    return (jnp.repeat(group_mean, channels // GROUPS), jnp.repeat(inv_scale, channels // GROUPS))


def normalize(values, group_mean, inv_scale, norm_gain, norm_shift):
    normed = (values.astype(jnp.float32) - group_mean) * inv_scale * norm_gain + norm_shift
    return jax.nn.silu(normed).astype(jnp.bfloat16)


def pad_block(local_block):
    previous = passed_along(local_block, "tm", 1)
    first_frame = jnp.broadcast_to(local_block[:1], previous.shape)
    previous = jnp.where(lax.axis_index("tm") == 0, first_frame, previous)
    extended = jnp.concatenate([previous, local_block], axis=0)
    padded = with_halo(extended, (("section", 2), ("tile", 1)), 1)
    upper_rim = jnp.where(lax.axis_index("tile") == 0, padded[:, 1:2], padded[:, :1])
    bottom = jnp.where(
        lax.axis_index("tile") == lax.axis_size("tile") - 1, padded[:, -2:-1], padded[:, -1:]
    )
    padded = jnp.concatenate([upper_rim, padded[:, 1:-1], bottom], axis=1)
    left_rim = jnp.where(lax.axis_index("section") == 0, padded[:, :, 1:2], padded[:, :, :1])
    right_rim = jnp.where(
        lax.axis_index("section") == lax.axis_size("section") - 1,
        padded[:, :, -2:-1],
        padded[:, :, -1:],
    )
    return jnp.concatenate([left_rim, padded[:, :, 1:-1], right_rim], axis=2)


def prepare(local_block, total_cells, norm_gain, norm_shift):
    group_mean, inv_scale = group_stats(local_block.astype(jnp.float32), total_cells)
    return pad_block(normalize(local_block, group_mean, inv_scale, norm_gain, norm_shift))


def convolve(padded, weights, conv_bias):
    frames = padded.shape[0] - 2
    row_count = padded.shape[1] - 2
    columns = padded.shape[2] - 2
    channels = weights.shape[3]
    outputs = weights.shape[4]
    summed = jnp.zeros((frames, row_count, columns, outputs), jnp.float32)
    for tap_t in range(3):
        for tap_h in range(3):
            time_slab = padded[tap_t : tap_t + frames, tap_h : tap_h + row_count]
            window = jnp.concatenate(
                [time_slab[:, :, tap_w : tap_w + columns] for tap_w in range(3)], axis=-1
            )
            kernel = weights[tap_t, tap_h].reshape(3 * channels, outputs)
            summed = summed + jnp.einsum(
                "frck,ko->frco", window, kernel, preferred_element_type=jnp.float32
            )
    return summed + conv_bias


def shards(
    features,
    norm_gain_in,
    norm_shift_in,
    conv_in_weight,
    conv_in_bias,
    norm_gain_mid,
    norm_shift_mid,
    conv_mid_weight,
    conv_mid_bias,
    skip_weight,
    skip_bias,
):
    local_block = lax.all_to_all(features, "section", split_axis=2, concat_axis=3, tiled=True)
    frames, row_count, columns, channels = local_block.shape
    total_cells = (
        frames
        * row_count
        * columns
        * lax.axis_size("section")
        * lax.axis_size("tm")
        * lax.axis_size("tile")
    )
    act_in = prepare(local_block, total_cells, norm_gain_in, norm_shift_in)
    hidden = convolve(act_in, conv_in_weight, conv_in_bias).astype(jnp.bfloat16)
    act_mid = prepare(hidden, total_cells, norm_gain_mid, norm_shift_mid)
    residual = convolve(act_mid, conv_mid_weight, conv_mid_bias)
    shortcut = (
        jnp.einsum("frck,ko->frco", local_block, skip_weight, preferred_element_type=jnp.float32)
        + skip_bias
    )
    return (residual + shortcut).astype(jnp.bfloat16)


def solution(mesh):
    in_specs = (P("tm", "tile", None, "section"), P(), P(), P(), P(), P(), P(), P(), P(), P(), P())
    out_specs = P("tm", "tile", "section", None)
    return jax.shard_map(shards, mesh=mesh, in_specs=in_specs, out_specs=out_specs, check_vma=False)
```

profile of v0, /device:TPU:1, one launch (start us, length us, event | category | flops | bytes accessed | tf_op | source)
XLA Modules:
  0.0 461.7 jit_solution(4556182296633790430)
XLA Ops:
  0.0 1.2 copy.14
  1.2 10.5 %all_to_all.18 = bf16[2,8,64,128]{3,1,0,2:T(8,128)(2,1)S(1)} all-to-all(bf16[2,8,64,128]{3,1,0,2:T(8,128)(2,1)S(1)} %copy.14), channel_id=1, replica_groups=mesh['section'=2,'tm'=32,'tile'=8] {'section'}, dimensions={2} | all-to-all | bytes 524288 | tf_op jit(solution)/shard_map/all_to_all | solution.py:108
  11.6 0.5 convert_reduce_fusion
  12.4 100.0 %psum.28 = f32[32]{0:T(128)S(1)} all-reduce(f32[32]{0:T(128)S(1)} %reduce_sum.51), channel_id=1, replica_groups=mesh['section'=2,'tm'=32,'tile'=8] {'section','tm','tile'}, use_global_device_ids=true, to_apply=%region_2.0 | all-reduce | flops 32 | bytes 256 | tf_op jit(solution)/shard_map/psum | solution.py:36
  112.6 0.6 fusion.56
  113.3 0.3 copy.40
  113.6 93.6 %psum.29 = f32[32]{0:T(128)S(1)} all-reduce(f32[32]{0:T(128)S(1)} %reduce_sum.54), channel_id=1, replica_groups=mesh['section'=2,'tm'=32,'tile'=8] {'section','tm','tile'}, use_global_device_ids=true, to_apply=%region_5.6 | all-reduce | flops 32 | bytes 256 | tf_op jit(solution)/shard_map/psum | solution.py:39
  207.8 0.2 multiply_convert_fusion
  208.0 2.8 collective-permute-start
  210.8 4.9 %collective-permute-done = bf16[2,8,32,256]{3,2,1,0:T(8,128)(2,1)S(1)} collective-permute-done((bf16[2,8,32,256]{3,2,1,0:T(8,128)(2,1)S(1)}, bf16[2,8,32,256]{3,2,1,0:T(8,128)(2,1)S(1)}, u32[]{:S(2)}, u32[]{:S(2)}) %collective-permute-start) | collective-permute-done | bytes 262176 | tf_op jit(solution)/shard_map/ppermute | solution.py:12
  215.8 1.3 collective-permute-start.1
  217.1 3.5 collective-permute-start.2
  220.6 0.8 collective-permute-done.2
  221.5 1.9 collective-permute-start.3
  223.4 1.5 collective-permute-done.3
  224.8 0.7 broadcast_select_fusion.4
  225.5 1.3 collective-permute-start.4
  226.8 1.1 fusion.157
  227.9 4.0 collective-permute-done.4
  231.9 0.4 pad_maximum_fusion
  232.3 0.3 slice.529
  232.7 0.5 fusion.114
  233.3 0.6 fusion.106
  233.9 0.5 pad_maximum_fusion.4
  234.4 0.5 fusion.159
  235.0 0.4 copy-done.8
  235.3 0.4 fusion.16
  235.9 0.4 convolution_add_fusion.16
  236.3 0.4 copy-done.6
  236.7 0.4 convolution_add_fusion.15
  237.1 0.2 copy-done.5
  237.3 0.4 convolution_add_fusion.14
  237.6 0.4 copy-done.4
  238.0 0.4 convolution_add_fusion.13
  238.4 0.6 copy-done.3
  238.9 0.4 convolution_add_fusion.12
  239.3 0.4 convolution_add_fusion.11
  239.7 0.4 convolution_add_fusion.10
  240.1 0.3 copy-done.14
  240.3 0.4 fusion.163
  241.0 102.1 %psum.30 = f32[32]{0:T(128)S(1)} all-reduce(f32[32]{0:T(128)S(1)} %reduce_sum.72), channel_id=1, replica_groups=mesh['section'=2,'tm'=32,'tile'=8] {'section','tm','tile'}, use_global_device_ids=true, to_apply=%region_8.9 | all-reduce | flops 32 | bytes 256 | tf_op jit(solution)/shard_map/psum | solution.py:36
  343.6 94.6 %psum.31 = f32[32]{0:T(128)S(1)} all-reduce(f32[32]{0:T(128)S(1)} %reduce_sum.75), channel_id=1, replica_groups=mesh['section'=2,'tm'=32,'tile'=8] {'section','tm','tile'}, use_global_device_ids=true, to_apply=%region_11.12 | all-reduce | flops 32 | bytes 256 | tf_op jit(solution)/shard_map/psum | solution.py:39
  438.5 1.5 collective-permute-start.5
  440.0 2.1 collective-permute-done.5
  442.2 1.3 collective-permute-start.6
  443.5 3.5 collective-permute-start.7
  447.0 0.8 collective-permute-done.7
  447.8 2.8 collective-permute-start.8
  450.6 1.1 collective-permute-done.8
  451.7 1.3 collective-permute-start.9
  453.1 3.7 collective-permute-done.9
  457.1 0.2 pad_maximum_fusion.9
  457.5 0.2 fusion.130
  457.8 0.3 fusion.122
  458.2 0.3 fusion.67
  458.5 0.3 convolution_add_fusion.8
  458.7 0.3 convolution_add_fusion.7
  459.0 0.3 convolution_add_fusion.6
  459.3 0.3 convolution_add_fusion.5
  459.5 0.3 convolution_add_fusion.4
  459.8 0.3 convolution_add_fusion.3
  460.1 0.3 convolution_add_fusion.2
  460.5 0.3 fusion.1
  460.8 0.9 fusion.3
  (74 shorter events, 3.6 us)
Async XLA Ops:
  0.0 460.8 %copy-start = (bf16[256,128]{1,0:T(8,128)(2,1)S(1)}, bf16[256,128]{1,0:T(8,128)(2,1)}, u32[]{:S(2)}) copy-start(bf16[256,128]{1,0:T(8,128)(2,1)} %param.20) | copy-start | bytes 196612
  0.0 207.7 %copy-start.10 = (f32[256]{0:T(256)S(1)}, f32[256]{0:T(256)}, u32[]{:S(2)}) copy-start(f32[256]{0:T(256)} %param.12) | copy-start | bytes 3076
  0.0 207.7 %copy-start.9 = (f32[256]{0:T(256)S(1)}, f32[256]{0:T(256)}, u32[]{:S(2)}) copy-start(f32[256]{0:T(256)} %param.13) | copy-start | bytes 3076
  208.0 18.9 %copy-start.1 = (bf16[3,3,3,256,128]{4,3,2,1,0:T(8,128)(2,1)S(1)}, bf16[3,3,3,256,128]{4,3,2,1,0:T(8,128)(2,1)}, u32[]{:S(2)}) copy-start(bf16[3,3,3,256,128]{4,3,2,1,0:T(8,128)(2,1)} %param.14) | copy-start | bytes 5308420
  208.0 7.8 %collective-permute-start = (bf16[2,8,32,256]{3,2,1,0:T(8,128)(2,1)S(1)}, bf16[2,8,32,256]{3,2,1,0:T(8,128)(2,1)S(1)}, u32[]{:S(2)}, u32[]{:S(2)}) collective-permute-start(bf16[2,8,32,256]{3,2,1,0:T(8,128)(2,1)S(1)} %multiply_convert_fusion), channel_id=1, source_target_pairs={{0,8},{8,16},{16,24},{24,32},{32,40},{40,48},{48,56},{56,64},{64,7... | collective-permute-start | bytes 786440 | tf_op jit(solution)/shard_map/ppermute | solution.py:12
  215.8 4.8 %collective-permute-start.1 = (bf16[4,8,1,256]{3,2,1,0:T(2,128)(2,1)S(1)}, bf16[4,8,1,256]{3,2,1,0:T(2,128)(2,1)S(1)}, u32[]{:S(2)}, u32[]{:S(2)}) collective-permute-start(bf16[4,8,1,256]{3,2,1,0:T(2,128)(2,1)S(1)} %get-tuple-element.51), channel_id=1, source_target_pairs={{0,256},{1,257},{2,258},{3,259},{4,260},{5,261},{6,262},{7,263},{8... | collective-permute-start | bytes 49160 | tf_op jit(solution)/shard_map/ppermute | solution.py:23
  217.1 4.3 collective-permute-start.2
  221.5 3.4 collective-permute-start.3
  225.5 6.3 %collective-permute-start.4 = (bf16[4,1,34,256]{3,2,1,0:T(8,128)(2,1)}, bf16[4,1,34,256]{3,2,1,0:T(8,128)(2,1)S(1)}, u32[]{:S(2)}, u32[]{:S(2)}) collective-permute-start(bf16[4,1,34,256]{3,2,1,0:T(8,128)(2,1)} %get-tuple-element.8), channel_id=1, source_target_pairs={{1,0},{2,1},{3,2},{4,3},{5,4},{6,5},{7,6},{9,8},{10,9},{11,10},{12... | collective-permute-start | bytes 208904 | tf_op jit(solution)/shard_map/ppermute | solution.py:25
  234.4 0.9 copy-start.8
  235.0 1.0 copy-start.7
  235.7 1.0 copy-start.6
  236.3 1.0 copy-start.5
  237.0 1.0 copy-start.4
  238.0 0.9 copy-start.3
  239.7 0.7 copy-start.14
  240.3 198.1 %copy-start.11 = (f32[128]{0:T(128)S(1)}, f32[128]{0:T(128)}, u32[]{:S(2)}) copy-start(f32[128]{0:T(128)} %param.17) | copy-start | bytes 1540
  240.3 198.1 %copy-start.12 = (f32[128]{0:T(128)S(1)}, f32[128]{0:T(128)}, u32[]{:S(2)}) copy-start(f32[128]{0:T(128)} %param.16) | copy-start | bytes 1540
  240.8 212.3 %copy-start.2 = (bf16[3,3,3,128,128]{4,3,2,1,0:T(8,128)(2,1)S(1)}, bf16[3,3,3,128,128]{4,3,2,1,0:T(8,128)(2,1)}, u32[]{:S(2)}) copy-start(bf16[3,3,3,128,128]{4,3,2,1,0:T(8,128)(2,1)} %param.18) | copy-start | bytes 2654212
  438.5 3.6 collective-permute-start.5
  442.2 4.8 %collective-permute-start.6 = (bf16[4,8,1,128]{3,2,1,0:T(2,128)(2,1)S(1)}, bf16[4,8,1,128]{3,2,1,0:T(2,128)(2,1)S(1)}, u32[]{:S(2)}, u32[]{:S(2)}) collective-permute-start(bf16[4,8,1,128]{3,2,1,0:T(2,128)(2,1)S(1)} %get-tuple-element.77), channel_id=1, source_target_pairs={{0,256},{1,257},{2,258},{3,259},{4,260},{5,261},{6,262},{7,263},{8... | collective-permute-start | bytes 24584 | tf_op jit(solution)/shard_map/ppermute | solution.py:23
  443.5 4.3 collective-permute-start.7
  447.8 3.9 collective-permute-start.8
  451.7 5.1 %collective-permute-start.9 = (bf16[4,1,34,128]{3,2,1,0:T(8,128)(2,1)S(1)}, bf16[4,1,34,128]{3,2,1,0:T(8,128)(2,1)S(1)}, u32[]{:S(2)}, u32[]{:S(2)}) collective-permute-start(bf16[4,1,34,128]{3,2,1,0:T(8,128)(2,1)S(1)} %get-tuple-element.6), channel_id=1, source_target_pairs={{1,0},{2,1},{3,2},{4,3},{5,4},{6,5},{7,6},{9,8},{10,9},{11,10},{12... | collective-permute-start | bytes 104456 | tf_op jit(solution)/shard_map/ppermute | solution.py:25
  459.8 0.7 copy-start.15
  460.1 0.7 copy-start.13
where the time goes:
time: 470 us; the launch traced here: 462 us
  blocking collectives  401 us (85%)
  starting transfers between devices  21.1 us (4%)
  waiting for transfers between devices  18.9 us (4%)
  local copies, waits for them, and re-layouts  7.64 us (2%)
  matrix products  6.65 us (1%)
  other arithmetic  6.07 us (1%)
    psum x2, blocking collectives, group_stats(): lax.psum(jnp.sum(grouped, axis=(0, 2)), ('section', 'tm', 'tile'))  202 us
    psum x2, blocking collectives, group_stats(): lax.psum(jnp.sum(centered * centered, axis=(0, 2)), ('section', 'tm', 'ti...  188 us
    all_to_all x1, blocking collectives, shards(): lax.all_to_all(features, 'section', split_axis=2, concat_axis=3, tiled=True)  10.5 us
    ppermute x4, starting transfers between devices, with_halo(): lax.ppermute(head, axis, [((i + 1) % count, i) for i in range(ends)])  9.49 us
  transfers between devices with their start and end apart: 10, of which 8 were waited for; matrix products, arithmetic and copies ran while one was open for 0% of the time, Pallas kernels for 0%

commit v1 on v0

v1 whole, which is shorter than its diff:
```python
import functools

import jax
import jax.numpy as jnp
from jax import lax
from jax.experimental import pallas as pl
from jax.experimental.pallas import tpu as pltpu
from jax.sharding import PartitionSpec as P

MESH = pl.DeviceIdType.MESH
EPS = 1e-06
F32 = jnp.float32
BF16 = jnp.bfloat16


def ring_distance(step, size):
    return min(step % size, (-step) % size)


def lane_group_sum(values, width):
    lanes = values.shape[-1]
    lane = lax.broadcasted_iota(jnp.int32, values.shape, values.ndim - 1)
    step = 1
    while step < width:
        upper = lax.rem(lane, 2 * step) >= step
        values = values + jnp.where(
            upper, pltpu.roll(values, step, 1), pltpu.roll(values, lanes - step, 1)
        )
        step *= 2
    return values


def combine(own, others, count):
    parts = others.shape[0] + 1
    total = own + jnp.sum(others, axis=0)
    mean = total * (1.0 / parts)
    spread = jnp.square(own - mean) + jnp.sum(jnp.square(others - mean[None]), axis=0)
    row = lax.broadcasted_iota(jnp.int32, own.shape, 0)
    return jnp.where(row == 0, mean, total + count * spread[0:1])


def silu(values):
    return values / (1.0 + jnp.exp(-values))


def kernel(
    sizes,
    features, gain_in, shift_in, w_in, b_in, gain_mid, shift_mid, w_mid, b_mid, w_skip, b_skip,
    out,
    x_ref, h_ref, act, w1, w2, ws, small,
    part_own, part_in, skip_own, skip_out, skip_in,
    stat_out, y_buf, xz_buf,
    load_sem, stat_send, stat_recv, halo_send, halo_recv, part_send, part_recv,
):
    nx, nz, ny = sizes
    s, tm, y = lax.axis_index("section"), lax.axis_index("tm"), lax.axis_index("tile")
    ntm = nx * nz
    x, z = tm // nz, lax.rem(tm, nz)
    frames, rows, cols, lanes = features.shape
    half = cols // 2
    wide = half + 16
    cells = frames * rows * cols

    def device(d_tm=None, d_y=0, plane=None, other=False):
        new_tm = tm
        if d_tm is not None:
            new_tm = lax.rem(tm + d_tm + ntm, ntm)
        if plane is not None:
            new_tm = lax.rem(x + plane[0], nx) * nz + lax.rem(z + plane[1], nz)
        new_y = lax.rem(y + d_y + ny, ny) if d_y else y
        return {"section": 1 - s if other else s, "tm": new_tm, "tile": new_y}

    y_steps = sorted(range(1, ny), key=lambda d: -ring_distance(d, ny))
    plane_steps = sorted(
        [(a, b) for a in range(nx) for b in range(nz) if (a, b) != (0, 0)],
        key=lambda d: -ring_distance(d[0], nx) - ring_distance(d[1], nz),
    )
    y_devices = [device(d_y=d) for d in y_steps]
    plane_devices = [device(plane=d) for d in plane_steps]
    partner = device(other=True)
    corner_devices = [device(d_tm=a, d_y=b) for a in (1, -1) for b in (1, -1)]

    barrier = pltpu.get_barrier_semaphore()
    greeted = plane_devices + y_devices + corner_devices + [partner]
    for peer in greeted:
        pl.semaphore_signal(barrier, inc=1, device_id=peer, device_id_type=MESH)

    own_frames, own_rows = pl.ds(frames, frames), pl.ds(1, rows)
    lower = pl.multiple_of(s * lanes, lanes)
    loads = [
        pltpu.make_async_copy(features, x_ref.at[own_frames, own_rows], load_sem.at[0]),
        pltpu.make_async_copy(w_skip.at[pl.ds(lower, lanes)], ws, load_sem.at[1]),
        pltpu.make_async_copy(w_in.at[:, :, :, pl.ds(lower, lanes)], w1, load_sem.at[2]),
        pltpu.make_async_copy(w_mid, w2, load_sem.at[3]),
    ]
    vectors = [gain_in.at[pl.ds(lower, lanes)], shift_in.at[pl.ds(lower, lanes)], b_in, gain_mid, shift_mid, b_mid, b_skip]
    for i, vector in enumerate(vectors):
        loads.append(pltpu.make_async_copy(vector, small.at[i], load_sem.at[4 + i]))
    for load in loads:
        load.start()

    def local_stats(ref, width):
        def add(i, total):
            block = ref[frames + i // rows, 1 + lax.rem(i, rows)].astype(F32)
            return total + jnp.sum(block.reshape(cols // 8, 8, lanes), axis=0)

        total = lax.fori_loop(0, frames * rows, add, jnp.zeros((8, lanes), F32), unroll=4)
        total = jnp.sum(total, axis=0, keepdims=True)
        mean = lane_group_sum(jnp.broadcast_to(total, (8, lanes)), width) * (1.0 / (cells * width))

        def add_square(i, total):
            block = ref[frames + i // rows, 1 + lax.rem(i, rows)].astype(F32).reshape(cols // 8, 8, lanes)
            return total + jnp.sum(jnp.square(block - mean[None]), axis=0)

        spread = lax.fori_loop(0, frames * rows, add_square, jnp.zeros((8, lanes), F32), unroll=4)
        spread = jnp.sum(spread, axis=0, keepdims=True)
        spread = lane_group_sum(jnp.broadcast_to(spread, (8, lanes)), width)
        row = lax.broadcasted_iota(jnp.int32, (8, lanes), 0)
        return jnp.where(row == 0, mean, spread)

    def stat_phase(which, tile, devices, buffer):
        stat_out[which] = tile
        for j, peer in enumerate(devices):
            pltpu.make_async_remote_copy(
                src_ref=stat_out.at[which], dst_ref=buffer.at[which // 2, j],
                send_sem=stat_send.at[which], recv_sem=stat_recv.at[which],
                device_id=peer, device_id_type=MESH,
            ).start()

    def stat_wait(which, buffer):
        received = buffer.at[which // 2]
        pltpu.make_async_copy(received, received, stat_recv.at[which]).wait()
        return received[...]

    def stat_done(which, buffer):
        received = buffer.at[which // 2]
        pltpu.make_async_copy(received, received, stat_send.at[which]).wait()

    def halos(ref, at_cols, base):
        last = rows
        moves = [
            ((own_frames, own_rows), (pl.ds(0, frames), own_rows), device(d_tm=1)),
            ((own_frames, last), (own_frames, 0), device(d_y=1)),
            ((own_frames, 1), (own_frames, rows + 1), device(d_y=-1)),
            ((own_frames, last), (pl.ds(0, frames), 0), device(d_tm=1, d_y=1)),
            ((own_frames, 1), (pl.ds(0, frames), rows + 1), device(d_tm=1, d_y=-1)),
        ]
        return [
            pltpu.make_async_remote_copy(
                src_ref=ref.at[(*source, at_cols)], dst_ref=ref.at[(*target, at_cols)],
                send_sem=halo_send.at[base + i], recv_sem=halo_recv.at[base + i],
                device_id=peer, device_id_type=MESH,
            )
            for i, (source, target, peer) in enumerate(moves)
        ]

    def scales(tile, count, gain, shift):
        mean, spread = tile[0:1], tile[1:2] * (1.0 / count)
        scale = lax.rsqrt(spread + EPS) * small[gain:gain + 1, :]
        return mean, scale, small[shift:shift + 1, :]

    def activate(ref, at_cols, width, mean, scale, shift):
        place = lax.broadcasted_iota(jnp.int32, (width, lanes), 0)

        def one(i, carry):
            f, r = i // (rows + 2), lax.rem(i, rows + 2)
            from_f = jnp.where(tm == 0, jnp.maximum(f, frames), f)
            from_r = jnp.where(y == 0, jnp.maximum(r, 1), r)
            from_r = jnp.where(y == ny - 1, jnp.minimum(from_r, rows), from_r)
            block = ref[from_f, from_r, at_cols].astype(F32)
            block = silu((block - mean) * scale + shift)
            left = jnp.where(place == 0, block, pltpu.roll(block, 1, 0))
            right = jnp.where(place == width - 1, block, pltpu.roll(block, width - 1, 0))
            act[0, f, r, 0:width] = left.astype(BF16)
            act[1, f, r, 0:width] = block.astype(BF16)
            act[2, f, r, 0:width] = right.astype(BF16)
            return carry

        lax.fori_loop(0, 2 * frames * (rows + 2), one, 0, unroll=2)

    def convolve(weights, f, r, n_rows, at_cols, n_cols):
        taps = [(t, i, j) for t in range(3) for i in range(3) for j in range(3)]
        windows = [
            act[j, f + t, pl.ds(r + i, n_rows), at_cols].reshape(n_rows * n_cols, lanes) for t, i, j in taps
        ]
        total = jnp.zeros((n_rows * n_cols, lanes), F32)
        for k in range(0, len(taps), 2):
            window = jnp.concatenate(windows[k:k + 2], axis=1)
            matrix = jnp.concatenate([weights[tap] for tap in taps[k:k + 2]], axis=0)
            total = total + jnp.dot(window, matrix, preferred_element_type=F32)
        return total

    loads[0].wait()
    tile = local_stats(x_ref, 8)
    pl.semaphore_wait(barrier, len(greeted))
    stat_phase(0, tile, y_devices, y_buf)
    feature_halos = halos(x_ref, slice(None), 0)
    for copy in feature_halos:
        copy.start()

    loads[1].wait()
    their_cols, our_cols = pl.multiple_of((1 - s) * half, half), pl.multiple_of(s * half, half)

    def skip_product(start):
        block = x_ref[own_frames, own_rows, pl.ds(start, half)].reshape(frames * rows * half, lanes)
        return jnp.dot(block, ws[...], preferred_element_type=F32)

    skip_out[...] = skip_product(their_cols)
    skip_copy = pltpu.make_async_remote_copy(
        src_ref=skip_out, dst_ref=skip_in, send_sem=part_send.at[0], recv_sem=part_recv.at[0],
        device_id=partner, device_id_type=MESH,
    )
    skip_copy.start()
    skip_own[...] = skip_product(our_cols)
    for load in loads[2:]:
        load.wait()

    tile = combine(tile, stat_wait(0, y_buf), float(cells * 8))
    stat_phase(1, tile, plane_devices, xz_buf)
    tile = combine(tile, stat_wait(1, xz_buf), float(cells * 8 * ny))
    mean, scale, shift = scales(tile, float(cells * 8 * ny * ntm), 0, 1)
    for copy in feature_halos:
        copy.wait_recv()
    activate(x_ref, slice(None), cols, mean, scale, shift)

    pieces = part_own.shape[0]
    piece_rows = rows * frames // pieces
    part_copies = [
        pltpu.make_async_remote_copy(
            src_ref=part_own.at[i], dst_ref=part_in.at[i],
            send_sem=part_send.at[1 + i], recv_sem=part_recv.at[1 + i],
            device_id=partner, device_id_type=MESH,
        )
        for i in range(pieces)
    ]
    for i in range(pieces):
        f, r = (i * piece_rows) // rows, (i * piece_rows) % rows
        part_own[i] = convolve(w1, f, r, piece_rows, slice(None), cols)
        part_copies[i].start()
    for i in range(pieces):
        f, r = (i * piece_rows) // rows, (i * piece_rows) % rows
        part_copies[i].wait_recv()
        hidden = part_own[i] + part_in[i] + small[2:3, :]
        h_ref[frames + f, 1 + r:1 + r + piece_rows] = hidden.astype(BF16).reshape(piece_rows, cols, lanes)

    tile = local_stats(h_ref, 4)
    stat_phase(2, tile, y_devices, y_buf)
    wide_start = pl.multiple_of(s * 16, 16)
    wide_cols = pl.ds(wide_start, wide)
    hidden_halos = halos(h_ref, wide_cols, len(feature_halos))
    for copy in hidden_halos:
        copy.start()
    skip_copy.wait_recv()
    skip_own[...] = skip_own[...] + skip_in[...] + (small[5:6, :] + small[6:7, :])
    tile = combine(tile, stat_wait(2, y_buf), float(cells * 4))
    stat_phase(3, tile, plane_devices, xz_buf)
    tile = combine(tile, stat_wait(3, xz_buf), float(cells * 4 * ny))
    mean, scale, shift = scales(tile, float(cells * 4 * ny * ntm), 3, 4)
    for copy in hidden_halos:
        copy.wait_recv()
    activate(h_ref, wide_cols, wide, mean, scale, shift)

    for f in range(frames):
        size = rows * half
        total = convolve(w2, f, 0, rows, pl.ds(wide_start, half), half)
        total = total + skip_own[f * size:(f + 1) * size, :]
        out[f] = total.astype(BF16).reshape(rows, half, lanes)

    for copy in feature_halos + hidden_halos + part_copies + [skip_copy]:
        copy.wait_send()
    for which, buffer in ((0, y_buf), (1, xz_buf), (2, y_buf), (3, xz_buf)):
        stat_done(which, buffer)


def shards(sizes, features, *others):
    nx, nz, ny = sizes
    frames, rows, cols, lanes = features.shape
    cells = frames * rows * cols
    pieces = 4
    dma = pltpu.SemaphoreType.DMA
    return pl.pallas_call(
        functools.partial(kernel, sizes),
        out_shape=jax.ShapeDtypeStruct((frames, rows, cols // 2, lanes), BF16),
        in_specs=[pl.BlockSpec(memory_space=pl.ANY)] * 11,
        out_specs=pl.BlockSpec(memory_space=pltpu.VMEM),
        scratch_shapes=[
            pltpu.VMEM((2 * frames, rows + 2, cols, lanes), BF16),
            pltpu.VMEM((2 * frames, rows + 2, cols, lanes), BF16),
            pltpu.VMEM((3, 2 * frames, rows + 2, cols, lanes), BF16),
            pltpu.VMEM((3, 3, 3, lanes, lanes), BF16),
            pltpu.VMEM((3, 3, 3, lanes, lanes), BF16),
            pltpu.VMEM((lanes, lanes), BF16),
            pltpu.VMEM((7, lanes), F32),
            pltpu.VMEM((pieces, cells // pieces, lanes), F32),
            pltpu.VMEM((pieces, cells // pieces, lanes), F32),
            pltpu.VMEM((cells // 2, lanes), F32),
            pltpu.VMEM((cells // 2, lanes), F32),
            pltpu.VMEM((cells // 2, lanes), F32),
            pltpu.VMEM((4, 8, lanes), F32),
            pltpu.VMEM((2, ny - 1, 8, lanes), F32),
            pltpu.VMEM((2, nx * nz - 1, 8, lanes), F32),
            dma((11,)), dma((4,)), dma((4,)), dma((10,)), dma((10,)), dma((pieces + 1,)), dma((pieces + 1,)),
        ],
        compiler_params=pltpu.CompilerParams(
            collective_id=0, has_side_effects=True, vmem_limit_bytes=40 * 2**20
        ),
        name="residual_block",
    )(features, *others)


def solution(mesh):
    nz = 8 if mesh.shape["tm"] % 8 == 0 else 2
    sizes = (mesh.shape["tm"] // nz, nz, mesh.shape["tile"])
    in_specs = (P("tm", "tile", None, "section"), P(), P(), P(), P(), P(), P(), P(), P(), P(), P())
    return jax.shard_map(
        functools.partial(shards, sizes), mesh=mesh, in_specs=in_specs,
        out_specs=P("tm", "tile", "section", None), check_vma=False,
    )
```

time: 470 us -> 58.1 us (0.12); the launches traced: 462 us -> 57.8 us
  blocking collectives: 401 us -> 0 us
  Pallas kernels: 0 us -> 48 us
  starting transfers between devices: 21.1 us -> 0 us
  waiting for transfers between devices: 18.9 us -> 0 us
  matrix products: 6.65 us -> 0 us
  other arithmetic: 6.07 us -> 0 us
    psum x4 -> x0, blocking collectives: 390 us -> none  [the longest x2 202 us: group_stats(): lax.psum(jnp.sum(grouped, axis=(0, 2)), ('section', 'tm', 'tile'))]
    pallas_call x0 -> x1, Pallas kernels: none -> 48 us  [shards(): pl.pallas_call(functools.partial(kernel, sizes), out_shape=jax.ShapeDtype...]
    ppermute x10 -> x0, starting transfers between devices: 21.1 us -> none  [the longest x4 9.49 us: with_halo(): lax.ppermute(head, axis, [((i + 1) % count, i) for i in range(ends)])]
    ppermute x10 -> x0, waiting for transfers between devices: 18.9 us -> none  [the longest x4 9.32 us: with_halo(): lax.ppermute(head, axis, [((i + 1) % count, i) for i in range(ends)])]
    all_to_all x1 -> x0, blocking collectives: 10.5 us -> none  [shards(): lax.all_to_all(features, 'section', split_axis=2, concat_axis=3, tiled=True)]
    dot_general x19 -> x0, matrix products: 6.65 us -> none  [the longest x18 5.76 us: convolve(): jnp.einsum('frck,ko->frco', window, kernel, preferred_element_type=jnp.fl...]
    unnamed x33 -> x23, local copies, waits for them, and re-layouts: 3.61 us -> 9.72 us
  transfers between devices with their start and end apart: 10 -> 0, of which waited for: 8 -> 0; matrix products, arithmetic and copies ran while one was open for 0% -> 0% of each run, Pallas kernels for 0% -> 0%
where the time goes in v1:
time: 58.1 us; the launch traced here: 57.8 us
  Pallas kernels  48 us (83%)
  local copies, waits for them, and re-layouts  9.72 us (17%)
    pallas_call x1, Pallas kernels, shards(): pl.pallas_call(functools.partial(kernel, sizes), out_shape=jax.ShapeDtype...  48 us
    unnamed x23, local copies, waits for them, and re-layouts  9.72 us

profile of v1, /device:TPU:1, one launch (start us, length us, event | category | flops | bytes accessed | tf_op | source)
XLA Modules:
  0.0 57.8 jit_solution(7084810274799933436)
XLA Ops:
  0.0 0.0 copy-start
  0.0 1.5 %copy-done = bf16[3,3,3,256,128]{4,3,2,1,0:T(8,128)(2,1)S(1)} copy-done((bf16[3,3,3,256,128]{4,3,2,1,0:T(8,128)(2,1)S(1)}, bf16[3,3,3,256,128]{4,3,2,1,0:T(8,128)(2,1)}, u32[]{:S(2)}) %copy-start) | copy-done | bytes 1769496
  1.5 0.0 copy-start.1
  1.5 1.2 %copy-done.1 = bf16[3,3,3,128,128]{4,3,2,1,0:T(8,128)(2,1)S(1)} copy-done((bf16[3,3,3,128,128]{4,3,2,1,0:T(8,128)(2,1)S(1)}, bf16[3,3,3,128,128]{4,3,2,1,0:T(8,128)(2,1)}, u32[]{:S(2)}) %copy-start.1) | copy-done | bytes 884760
  2.6 0.0 copy-start.2
  2.6 0.9 %copy-done.2 = bf16[2,8,64,128]{3,2,1,0:T(8,128)(2,1)S(1)} copy-done((bf16[2,8,64,128]{3,2,1,0:T(8,128)(2,1)S(1)}, bf16[2,8,64,128]{3,2,1,0:T(8,128)(2,1)}, u32[]{:S(2)}) %copy-start.2) | copy-done | bytes 262168
  3.6 0.0 copy-start.3
  3.6 0.8 %copy-done.3 = bf16[256,128]{1,0:T(8,128)(2,1)S(1)} copy-done((bf16[256,128]{1,0:T(8,128)(2,1)S(1)}, bf16[256,128]{1,0:T(8,128)(2,1)}, u32[]{:S(2)}) %copy-start.3) | copy-done | bytes 65560
  4.4 0.0 copy-start.4
  4.4 0.7 %copy-done.4 = f32[256]{0:T(256)S(1)} copy-done((f32[256]{0:T(256)S(1)}, f32[256]{0:T(256)}, u32[]{:S(2)}) %copy-start.4) | copy-done | bytes 1048
  5.1 0.0 copy-start.5
  5.1 0.7 %copy-done.5 = f32[256]{0:T(256)S(1)} copy-done((f32[256]{0:T(256)S(1)}, f32[256]{0:T(256)}, u32[]{:S(2)}) %copy-start.5) | copy-done | bytes 1048
  5.8 0.0 copy-start.6
  5.8 0.7 %copy-done.6 = f32[128]{0:T(128)S(1)} copy-done((f32[128]{0:T(128)S(1)}, f32[128]{0:T(128)}, u32[]{:S(2)}) %copy-start.6) | copy-done | bytes 536
  6.5 0.0 copy-start.7
  6.5 0.7 %copy-done.7 = f32[128]{0:T(128)S(1)} copy-done((f32[128]{0:T(128)S(1)}, f32[128]{0:T(128)}, u32[]{:S(2)}) %copy-start.7) | copy-done | bytes 536
  7.1 0.0 copy-start.8
  7.1 0.7 %copy-done.8 = f32[128]{0:T(128)S(1)} copy-done((f32[128]{0:T(128)S(1)}, f32[128]{0:T(128)}, u32[]{:S(2)}) %copy-start.8) | copy-done | bytes 536
  7.8 0.0 copy-start.9
  7.8 0.7 %copy-done.9 = f32[128]{0:T(128)S(1)} copy-done((f32[128]{0:T(128)S(1)}, f32[128]{0:T(128)}, u32[]{:S(2)}) %copy-start.9) | copy-done | bytes 536
  8.4 0.0 copy-start.10
  8.4 0.7 %copy-done.10 = f32[128]{0:T(128)S(1)} copy-done((f32[128]{0:T(128)S(1)}, f32[128]{0:T(128)}, u32[]{:S(2)}) %copy-start.10) | copy-done | bytes 536
  9.1 48.0 %residual_block.1 = bf16[2,8,32,128]{3,2,1,0:T(8,128)(2,1)S(1)} custom-call(bf16[2,8,64,128]{3,2,1,0:T(8,128)(2,1)S(1)} %copy-done.2, f32[256]{0:T(256)S(1)} %copy-done.4, f32[256]{0:T(256)S(1)} %copy-done.5, bf16[3,3,3,256,128]{4,3,2,1,0:T(8,128)(2,1)S(1)} %copy-done, f32[128]{0:T(128)S(1)} %copy-done.6, f32[128]{0:T(128)S(1)} %copy-done.7, ...), custom_call_target="tpu_custom_call" | custom-call | tf_op jit(solution)/shard_map/residual_block/pallas_call | solution.py:281
  57.1 0.7 %copy.13 = bf16[2,8,32,128]{3,2,1,0:T(8,128)(2,1)} copy(bf16[2,8,32,128]{3,2,1,0:T(8,128)(2,1)S(1)} %residual_block.1) | data formatting | bytes 262144
Async XLA Ops:
  0.0 1.5 %copy-start = (bf16[3,3,3,256,128]{4,3,2,1,0:T(8,128)(2,1)S(1)}, bf16[3,3,3,256,128]{4,3,2,1,0:T(8,128)(2,1)}, u32[]{:S(2)}) copy-start(bf16[3,3,3,256,128]{4,3,2,1,0:T(8,128)(2,1)} %w_in.1) | copy-start | bytes 5308420
  1.5 1.2 %copy-start.1 = (bf16[3,3,3,128,128]{4,3,2,1,0:T(8,128)(2,1)S(1)}, bf16[3,3,3,128,128]{4,3,2,1,0:T(8,128)(2,1)}, u32[]{:S(2)}) copy-start(bf16[3,3,3,128,128]{4,3,2,1,0:T(8,128)(2,1)} %w_mid.1) | copy-start | bytes 2654212
  2.6 0.9 %copy-start.2 = (bf16[2,8,64,128]{3,2,1,0:T(8,128)(2,1)S(1)}, bf16[2,8,64,128]{3,2,1,0:T(8,128)(2,1)}, u32[]{:S(2)}) copy-start(bf16[2,8,64,128]{3,2,1,0:T(8,128)(2,1)} %features.1) | copy-start | bytes 786436
  3.6 0.8 %copy-start.3 = (bf16[256,128]{1,0:T(8,128)(2,1)S(1)}, bf16[256,128]{1,0:T(8,128)(2,1)}, u32[]{:S(2)}) copy-start(bf16[256,128]{1,0:T(8,128)(2,1)} %w_skip.1) | copy-start | bytes 196612
  4.4 0.7 %copy-start.4 = (f32[256]{0:T(256)S(1)}, f32[256]{0:T(256)}, u32[]{:S(2)}) copy-start(f32[256]{0:T(256)} %gain_in.1) | copy-start | bytes 3076
  5.1 0.7 %copy-start.5 = (f32[256]{0:T(256)S(1)}, f32[256]{0:T(256)}, u32[]{:S(2)}) copy-start(f32[256]{0:T(256)} %shift_in.1) | copy-start | bytes 3076
  5.8 0.7 %copy-start.6 = (f32[128]{0:T(128)S(1)}, f32[128]{0:T(128)}, u32[]{:S(2)}) copy-start(f32[128]{0:T(128)} %b_in.1) | copy-start | bytes 1540
  6.5 0.7 %copy-start.7 = (f32[128]{0:T(128)S(1)}, f32[128]{0:T(128)}, u32[]{:S(2)}) copy-start(f32[128]{0:T(128)} %gain_mid.1) | copy-start | bytes 1540
  7.1 0.7 %copy-start.8 = (f32[128]{0:T(128)S(1)}, f32[128]{0:T(128)}, u32[]{:S(2)}) copy-start(f32[128]{0:T(128)} %shift_mid.1) | copy-start | bytes 1540
  7.8 0.7 %copy-start.9 = (f32[128]{0:T(128)S(1)}, f32[128]{0:T(128)}, u32[]{:S(2)}) copy-start(f32[128]{0:T(128)} %b_mid.1) | copy-start | bytes 1540
  8.4 0.7 %copy-start.10 = (f32[128]{0:T(128)S(1)}, f32[128]{0:T(128)}, u32[]{:S(2)}) copy-start(f32[128]{0:T(128)} %b_skip.1) | copy-start | bytes 1540

commit v2 on v1

--- a/solution.py
+++ b/solution.py
@@ -225,23 +225,30 @@
 
     pieces = part_own.shape[0]
     piece_rows = rows * frames // pieces
-    part_copies = [
-        pltpu.make_async_remote_copy(
+
+    def part_copy(i):
+        return pltpu.make_async_remote_copy(
             src_ref=part_own.at[i], dst_ref=part_in.at[i],
             send_sem=part_send.at[1 + i], recv_sem=part_recv.at[1 + i],
             device_id=partner, device_id_type=MESH,
         )
-        for i in range(pieces)
-    ]
-    for i in range(pieces):
-        f, r = (i * piece_rows) // rows, (i * piece_rows) % rows
+
+    def first_piece(i, carry):
+        f, r = (i * piece_rows) // rows, lax.rem(i * piece_rows, rows)
         part_own[i] = convolve(w1, f, r, piece_rows, slice(None), cols)
-        part_copies[i].start()
-    for i in range(pieces):
-        f, r = (i * piece_rows) // rows, (i * piece_rows) % rows
-        part_copies[i].wait_recv()
+        part_copy(i).start()
+        return carry
+
+    lax.fori_loop(0, pieces, first_piece, 0)
+
+    def hidden_piece(i, carry):
+        f, r = (i * piece_rows) // rows, lax.rem(i * piece_rows, rows)
+        part_copy(i).wait_recv()
         hidden = part_own[i] + part_in[i] + small[2:3, :]
-        h_ref[frames + f, 1 + r:1 + r + piece_rows] = hidden.astype(BF16).reshape(piece_rows, cols, lanes)
+        h_ref[frames + f, pl.ds(1 + r, piece_rows)] = hidden.astype(BF16).reshape(piece_rows, cols, lanes)
+        return carry
+
+    lax.fori_loop(0, pieces, hidden_piece, 0)
 
     tile = local_stats(h_ref, 4)
     stat_phase(2, tile, y_devices, y_buf)
@@ -260,13 +267,16 @@
         copy.wait_recv()
     activate(h_ref, wide_cols, wide, mean, scale, shift)
 
-    for f in range(frames):
+    def second_piece(f, carry):
         size = rows * half
         total = convolve(w2, f, 0, rows, pl.ds(wide_start, half), half)
-        total = total + skip_own[f * size:(f + 1) * size, :]
+        total = total + skip_own[pl.ds(pl.multiple_of(f * size, size), size), :]
         out[f] = total.astype(BF16).reshape(rows, half, lanes)
-
-    for copy in feature_halos + hidden_halos + part_copies + [skip_copy]:
+        return carry
+
+    lax.fori_loop(0, frames, second_piece, 0)
+
+    for copy in feature_halos + hidden_halos + [skip_copy] + [part_copy(i) for i in range(pieces)]:
         copy.wait_send()
     for which, buffer in ((0, y_buf), (1, xz_buf), (2, y_buf), (3, xz_buf)):
         stat_done(which, buffer)
@@ -281,7 +291,7 @@
     return pl.pallas_call(
         functools.partial(kernel, sizes),
         out_shape=jax.ShapeDtypeStruct((frames, rows, cols // 2, lanes), BF16),
-        in_specs=[pl.BlockSpec(memory_space=pl.ANY)] * 11,
+        in_specs=[pl.BlockSpec(memory_space=pltpu.HBM)] * 11,
         out_specs=pl.BlockSpec(memory_space=pltpu.VMEM),
         scratch_shapes=[
             pltpu.VMEM((2 * frames, rows + 2, cols, lanes), BF16),
@@ -305,7 +315,7 @@
             collective_id=0, has_side_effects=True, vmem_limit_bytes=40 * 2**20
         ),
         name="residual_block",
-    )(features, *others)
+    )(*[pltpu.with_memory_space_constraint(array, pltpu.HBM) for array in (features, *others)])
 
 
 def solution(mesh):

time: 58.1 us -> 48.8 us (0.84)
  local copies, waits for them, and re-layouts: 9.72 us -> 0.66 us
    unnamed x23 -> x1, local copies, waits for them, and re-layouts: 9.72 us -> 0.66 us
where the time goes in v2:
time: 48.8 us; the launch traced here: 48.6 us
  Pallas kernels  48 us (98%)
  local copies, waits for them, and re-layouts  0.66 us (1%)
    pallas_call x1, Pallas kernels, shards(): pl.pallas_call(functools.partial(kernel, sizes), out_shape=jax.ShapeDtype...  48 us

profile of v2, /device:TPU:1, one launch (start us, length us, event | category | flops | bytes accessed | tf_op | source)
XLA Modules:
  0.0 48.6 jit_solution(7260375197372303257)
XLA Ops:
  0.0 48.0 %residual_block.1 = bf16[2,8,32,128]{3,2,1,0:T(8,128)(2,1)S(1)} custom-call(bf16[2,8,64,128]{3,2,1,0:T(8,128)(2,1)} %features.1, f32[256]{0:T(256)} %gain_in.1, f32[256]{0:T(256)} %shift_in.1, bf16[3,3,3,256,128]{4,3,2,1,0:T(8,128)(2,1)} %w_in.1, f32[128]{0:T(128)} %b_in.1, f32[128]{0:T(128)} %gain_mid.1, f32[128]{0:T(128)} %shift_mid.1, ...), custom_call_target="tpu_custom_call" | custom-call | tf_op jit(solution)/shard_map/residual_block/pallas_call | solution.py:291
  48.0 0.7 %copy.13 = bf16[2,8,32,128]{3,2,1,0:T(8,128)(2,1)} copy(bf16[2,8,32,128]{3,2,1,0:T(8,128)(2,1)S(1)} %residual_block.1) | data formatting | bytes 262144

commit v3 on v2

--- a/solution.py
+++ b/solution.py
@@ -40,7 +40,8 @@
 
 
 def silu(values):
-    return values / (1.0 + jnp.exp(-values))
+    halved = 0.5 * values
+    return halved + halved * jnp.tanh(halved)
 
 
 def kernel(
@@ -66,22 +67,31 @@
         if d_tm is not None:
             new_tm = lax.rem(tm + d_tm + ntm, ntm)
         if plane is not None:
-            new_tm = lax.rem(x + plane[0], nx) * nz + lax.rem(z + plane[1], nz)
+            new_tm = plane[0] * nz + lax.rem(z + plane[1], nz)
         new_y = lax.rem(y + d_y + ny, ny) if d_y else y
         return {"section": 1 - s if other else s, "tm": new_tm, "tile": new_y}
 
-    y_steps = sorted(range(1, ny), key=lambda d: -ring_distance(d, ny))
-    plane_steps = sorted(
-        [(a, b) for a in range(nx) for b in range(nz) if (a, b) != (0, 0)],
-        key=lambda d: -ring_distance(d[0], nx) - ring_distance(d[1], nz),
-    )
-    y_devices = [device(d_y=d) for d in y_steps]
-    plane_devices = [device(plane=d) for d in plane_steps]
+    near = x + 1 - 2 * lax.rem(x, 2)
+    far = nx - 1 - x
+    y_devices = [
+        device(d_y=d, plane=(to_x, 0))
+        for d, to_x in sorted(
+            [(d, to_x) for d in range(ny) for to_x in (x, near) if d or to_x is near],
+            key=lambda pair: -ring_distance(pair[0], ny),
+        )
+    ]
+    plane_devices = [
+        device(plane=(to_x, d))
+        for d, to_x in sorted(
+            [(d, to_x) for d in range(nz) for to_x in (x, far) if d or to_x is far],
+            key=lambda pair: -ring_distance(pair[0], nz),
+        )
+    ]
     partner = device(other=True)
     corner_devices = [device(d_tm=a, d_y=b) for a in (1, -1) for b in (1, -1)]
 
     barrier = pltpu.get_barrier_semaphore()
-    greeted = plane_devices + y_devices + corner_devices + [partner]
+    greeted = plane_devices + y_devices + corner_devices + [device(d_tm=1), device(d_tm=-1), partner]
     for peer in greeted:
         pl.semaphore_signal(barrier, inc=1, device_id=peer, device_id_type=MESH)
 
@@ -217,7 +227,7 @@
 
     tile = combine(tile, stat_wait(0, y_buf), float(cells * 8))
     stat_phase(1, tile, plane_devices, xz_buf)
-    tile = combine(tile, stat_wait(1, xz_buf), float(cells * 8 * ny))
+    tile = combine(tile, stat_wait(1, xz_buf), float(cells * 8 * 2 * ny))
     mean, scale, shift = scales(tile, float(cells * 8 * ny * ntm), 0, 1)
     for copy in feature_halos:
         copy.wait_recv()
@@ -261,7 +271,7 @@
     skip_own[...] = skip_own[...] + skip_in[...] + (small[5:6, :] + small[6:7, :])
     tile = combine(tile, stat_wait(2, y_buf), float(cells * 4))
     stat_phase(3, tile, plane_devices, xz_buf)
-    tile = combine(tile, stat_wait(3, xz_buf), float(cells * 4 * ny))
+    tile = combine(tile, stat_wait(3, xz_buf), float(cells * 4 * 2 * ny))
     mean, scale, shift = scales(tile, float(cells * 4 * ny * ntm), 3, 4)
     for copy in hidden_halos:
         copy.wait_recv()
@@ -307,8 +317,8 @@
             pltpu.VMEM((cells // 2, lanes), F32),
             pltpu.VMEM((cells // 2, lanes), F32),
             pltpu.VMEM((4, 8, lanes), F32),
-            pltpu.VMEM((2, ny - 1, 8, lanes), F32),
-            pltpu.VMEM((2, nx * nz - 1, 8, lanes), F32),
+            pltpu.VMEM((2, 2 * ny - 1, 8, lanes), F32),
+            pltpu.VMEM((2, 2 * nz - 1, 8, lanes), F32),
             dma((11,)), dma((4,)), dma((4,)), dma((10,)), dma((10,)), dma((pieces + 1,)), dma((pieces + 1,)),
         ],
         compiler_params=pltpu.CompilerParams(

time: 48.8 us -> 46.6 us (0.955)
  Pallas kernels: 48 us -> 45.8 us
    pallas_call x1, Pallas kernels: 48 us -> 45.8 us  [shards(): pl.pallas_call(functools.partial(kernel, sizes), out_shape=jax.ShapeDtype...]
where the time goes in v3:
time: 46.6 us; the launch traced here: 46.5 us
  Pallas kernels  45.8 us (98%)
  local copies, waits for them, and re-layouts  0.66 us (1%)
    pallas_call x1, Pallas kernels, shards(): pl.pallas_call(functools.partial(kernel, sizes), out_shape=jax.ShapeDtype...  45.8 us

profile of v3, /device:TPU:1, one launch (start us, length us, event | category | flops | bytes accessed | tf_op | source)
XLA Modules:
  0.0 46.5 jit_solution(10096063835591751796)
XLA Ops:
  0.0 45.8 %residual_block.1 = bf16[2,8,32,128]{3,2,1,0:T(8,128)(2,1)S(1)} custom-call(bf16[2,8,64,128]{3,2,1,0:T(8,128)(2,1)} %features.1, f32[256]{0:T(256)} %gain_in.1, f32[256]{0:T(256)} %shift_in.1, bf16[3,3,3,256,128]{4,3,2,1,0:T(8,128)(2,1)} %w_in.1, f32[128]{0:T(128)} %b_in.1, f32[128]{0:T(128)} %gain_mid.1, f32[128]{0:T(128)} %shift_mid.1, ...), custom_call_target="tpu_custom_call" | custom-call | tf_op jit(solution)/shard_map/residual_block/pallas_call | solution.py:301
  45.8 0.7 %copy.13 = bf16[2,8,32,128]{3,2,1,0:T(8,128)(2,1)} copy(bf16[2,8,32,128]{3,2,1,0:T(8,128)(2,1)S(1)} %residual_block.1) | data formatting | bytes 262144

commit v4 on v3

--- a/solution.py
+++ b/solution.py
@@ -92,9 +92,6 @@
 
     barrier = pltpu.get_barrier_semaphore()
     greeted = plane_devices + y_devices + corner_devices + [device(d_tm=1), device(d_tm=-1), partner]
-    for peer in greeted:
-        pl.semaphore_signal(barrier, inc=1, device_id=peer, device_id_type=MESH)
-
     own_frames, own_rows = pl.ds(frames, frames), pl.ds(1, rows)
     lower = pl.multiple_of(s * lanes, lanes)
     loads = [
@@ -106,7 +103,10 @@
     vectors = [gain_in.at[pl.ds(lower, lanes)], shift_in.at[pl.ds(lower, lanes)], b_in, gain_mid, shift_mid, b_mid, b_skip]
     for i, vector in enumerate(vectors):
         loads.append(pltpu.make_async_copy(vector, small.at[i], load_sem.at[4 + i]))
-    for load in loads:
+    loads[0].start()
+    for peer in greeted:
+        pl.semaphore_signal(barrier, inc=1, device_id=peer, device_id_type=MESH)
+    for load in loads[1:]:
         load.start()
 
     def local_stats(ref, width):
@@ -114,7 +114,7 @@
             block = ref[frames + i // rows, 1 + lax.rem(i, rows)].astype(F32)
             return total + jnp.sum(block.reshape(cols // 8, 8, lanes), axis=0)
 
-        total = lax.fori_loop(0, frames * rows, add, jnp.zeros((8, lanes), F32), unroll=4)
+        total = lax.fori_loop(0, frames * rows, add, jnp.zeros((8, lanes), F32), unroll=16)
         total = jnp.sum(total, axis=0, keepdims=True)
         mean = lane_group_sum(jnp.broadcast_to(total, (8, lanes)), width) * (1.0 / (cells * width))
 
@@ -122,7 +122,7 @@
             block = ref[frames + i // rows, 1 + lax.rem(i, rows)].astype(F32).reshape(cols // 8, 8, lanes)
             return total + jnp.sum(jnp.square(block - mean[None]), axis=0)
 
-        spread = lax.fori_loop(0, frames * rows, add_square, jnp.zeros((8, lanes), F32), unroll=4)
+        spread = lax.fori_loop(0, frames * rows, add_square, jnp.zeros((8, lanes), F32), unroll=16)
         spread = jnp.sum(spread, axis=0, keepdims=True)
         spread = lane_group_sum(jnp.broadcast_to(spread, (8, lanes)), width)
         row = lax.broadcasted_iota(jnp.int32, (8, lanes), 0)
@@ -186,7 +186,7 @@
             act[2, f, r, 0:width] = right.astype(BF16)
             return carry
 
-        lax.fori_loop(0, 2 * frames * (rows + 2), one, 0, unroll=2)
+        lax.fori_loop(0, 2 * frames * (rows + 2), one, 0, unroll=8)
 
     def convolve(weights, f, r, n_rows, at_cols, n_cols):
         taps = [(t, i, j) for t in range(3) for i in range(3) for j in range(3)]

time: 46.6 us -> 45.7 us (0.981)
  Pallas kernels: 45.8 us -> 44.9 us
    pallas_call x1, Pallas kernels: 45.8 us -> 44.9 us  [shards(): pl.pallas_call(functools.partial(kernel, sizes), out_shape=jax.ShapeDtype...]
where the time goes in v4:
time: 45.7 us; the launch traced here: 45.6 us
  Pallas kernels  44.9 us (98%)
  local copies, waits for them, and re-layouts  0.66 us (1%)
    pallas_call x1, Pallas kernels, shards(): pl.pallas_call(functools.partial(kernel, sizes), out_shape=jax.ShapeDtype...  44.9 us

profile of v4, /device:TPU:1, one launch (start us, length us, event | category | flops | bytes accessed | tf_op | source)
XLA Modules:
  0.0 45.6 jit_solution(5730919919571316018)
XLA Ops:
  0.0 44.9 %residual_block.1 = bf16[2,8,32,128]{3,2,1,0:T(8,128)(2,1)S(1)} custom-call(bf16[2,8,64,128]{3,2,1,0:T(8,128)(2,1)} %features.1, f32[256]{0:T(256)} %gain_in.1, f32[256]{0:T(256)} %shift_in.1, bf16[3,3,3,256,128]{4,3,2,1,0:T(8,128)(2,1)} %w_in.1, f32[128]{0:T(128)} %b_in.1, f32[128]{0:T(128)} %gain_mid.1, f32[128]{0:T(128)} %shift_mid.1, ...), custom_call_target="tpu_custom_call" | custom-call | tf_op jit(solution)/shard_map/residual_block/pallas_call | solution.py:301
  44.9 0.7 %copy.13 = bf16[2,8,32,128]{3,2,1,0:T(8,128)(2,1)} copy(bf16[2,8,32,128]{3,2,1,0:T(8,128)(2,1)S(1)} %residual_block.1) | data formatting | bytes 262144
